TPU v7x, 32 devices: a whole 2x2x4 slice. The times are simulated.
32 devices in a mesh: freq: 4 (over x, core), rcv: 8 (over z, y).
Axes of the slice: x: 2, y: 2, z: 4, core: 2. Of those that a mesh axis runs over, the one named last changes fastest.
Arguments:
- reflection: bfloat16 [8, 2, 2560, 2560], P('freq', None, 'rcv'), may hold values from -5 to 5, as said below
- starts: int32 [2560, 192], P('rcv'), may hold values from 8 to 56
- focusing: float32 [8, 2560, 2, 192], P('freq', 'rcv'), may hold values from -6 to 6
- residual: float32 [8, 2560, 2, 192], P('freq', 'rcv'), may hold values from -6 to 6
- direction: float32 [8, 2560, 2, 192], P('freq', 'rcv'), may hold values from -6 to 6
- gradient: float32 [8, 2560, 2, 192], P('freq', 'rcv'), may hold values from -30 to 30
Outputs:
- new_focusing: float32 [8, 2560, 2, 192], P('freq', 'rcv')
- new_residual: float32 [8, 2560, 2, 192], P('freq', 'rcv')
- new_direction: float32 [8, 2560, 2, 192], P('freq', 'rcv')
- green_field: float32 [8, 2560, 2, 192], P('freq', 'rcv')
- focal_correlation: float32 [8, 2, 192], P('freq')
Inputs may be any that keep to these rules, and one draw needn't show every extreme that they name: Each frequency's matrix is symmetric in source and receiver: reflection[f, c, s, r] = reflection[f, c, r, s].
All inputs are finite; a program needn't handle non-finite values.
Results may differ from a plain program's by a relative error of at most 0.0003.
The roundings to bfloat16 on the way count: a program that leaves them out, or rounds other values in their place, can miss the bound.
Values may be sent and summed in bfloat16 or wider, within the bound.
No kernel may reach another device: no remote copies, remote signals or barrier semaphores. Data moves between devices by JAX's collectives and lax.ppermute only.
A program may use at most 64 MiB of HBM per device.

v0:
```python
import math
import jax
import jax.numpy as jnp
from jax import lax
from jax.sharding import PartitionSpec as P

N = 2560
F = 8
TS = 64
band_start = 5
tiny = 1e-06
highest = lax.Precision.HIGHEST


def tables(count):
    times = jnp.arange(TS, dtype=jnp.float32)[:, None]
    bins = (jnp.arange(count, dtype=jnp.int32) + band_start).astype(jnp.float32)[None, :]
    phase = 2.0 * jnp.pi * times * bins / TS
    return (jnp.cos(phase), jnp.sin(phase))


def contract_time(table, values):
    return jnp.einsum("tf,frk->trk", table, values, precision=highest)


def contract_back(table, values):
    return jnp.einsum("tf,trk->frk", table, values, precision=highest)


def time_gate(field, forward_cos, forward_sin, back_cos, back_sin, limits, complement):
    real_part = field[:, :, 0]
    imag_part = field[:, :, 1]
    time_real = contract_time(forward_cos, real_part) - contract_time(forward_sin, imag_part)
    time_imag = contract_time(forward_sin, real_part) + contract_time(forward_cos, imag_part)
    clock = jnp.arange(TS, dtype=jnp.int32)[:, None, None]
    window = (clock < limits[None]).astype(jnp.float32)
    if complement:
        window = 1.0 - window
    kept_real = window * time_real
    kept_imag = window * time_imag
    out_real = (contract_back(back_cos, kept_real) + contract_back(back_sin, kept_imag)) / TS
    out_imag = (contract_back(back_cos, kept_imag) - contract_back(back_sin, kept_real)) / TS
    return jnp.stack([out_real, out_imag], axis=2)


def combine(total, conjugate):
    if conjugate:
        out_real = total[:, 0, :, 0] + total[:, 1, :, 1]
        out_imag = total[:, 0, :, 1] - total[:, 1, :, 0]
    else:
        out_real = total[:, 0, :, 0] - total[:, 1, :, 1]
        out_imag = total[:, 0, :, 1] + total[:, 1, :, 0]
    return jnp.stack([out_real, out_imag], axis=2)


def per_device(reflection, starts, focusing, residual, direction, gradient):
    local_rows = reflection.shape[2]
    groups = lax.axis_size("freq")
    position = lax.axis_index("freq")
    cos_table, sin_table = tables(F)

    def gate(field, complement):
        spread = lax.all_to_all(field, "freq", split_axis=1, concat_axis=0, tiled=True)
        share = local_rows // groups
        limits = lax.dynamic_slice_in_dim(starts, position * share, share, 0)
        gated_part = time_gate(
            spread, cos_table, sin_table, cos_table, sin_table, limits, complement
        )
        return lax.all_to_all(gated_part, "freq", split_axis=0, concat_axis=1, tiled=True)

    def accumulate(piece):
        return jnp.einsum("fpnm,fmqk->fpnqk", reflection, piece, preferred_element_type=jnp.float32)

    direction_low = direction.astype(jnp.bfloat16)
    focusing_low = focusing.astype(jnp.bfloat16)
    aimed_total = accumulate(lax.all_gather(direction_low, "rcv", axis=1, tiled=True))
    direction_image = combine(aimed_total, False)
    gamma = lax.psum(jnp.sum(gradient * gradient), ("freq", "rcv"))
    image = gate(direction_image, False)
    curvature = lax.psum(jnp.sum(image * image), ("freq", "rcv"))
    alpha = gamma / (curvature + tiny)
    new_focusing = focusing + alpha * direction
    new_residual = residual - alpha * image
    gated = gate(new_residual, False).astype(jnp.bfloat16)
    total = accumulate(lax.all_gather(gated, "rcv", axis=1, tiled=True))
    new_gradient = combine(total, True)
    new_gamma = lax.psum(jnp.sum(new_gradient * new_gradient), ("freq", "rcv"))
    new_direction = new_gradient + new_gamma / (gamma + tiny) * direction
    focus_total = accumulate(lax.all_gather(focusing_low, "rcv", axis=1, tiled=True))
    focusing_image = combine(focus_total, False)
    green_field = gate(focusing_image + alpha * direction_image, True)
    corr_real = jnp.sum(
        green_field[:, :, 0] * new_focusing[:, :, 0] + green_field[:, :, 1] * new_focusing[:, :, 1],
        axis=1,
    )
    corr_imag = jnp.sum(
        green_field[:, :, 1] * new_focusing[:, :, 0] - green_field[:, :, 0] * new_focusing[:, :, 1],
        axis=1,
    )
    partial_corr = jnp.stack([corr_real, corr_imag], axis=1)
    focal_correlation = lax.psum(partial_corr, "rcv") / math.sqrt(N)
    return (new_focusing, new_residual, new_direction, green_field, focal_correlation)


def solution(mesh):
    return jax.shard_map(
        per_device,
        mesh=mesh,
        in_specs=(
            P("freq", None, "rcv", None),
            P("rcv", None),
            P("freq", "rcv", None, None),
            P("freq", "rcv", None, None),
            P("freq", "rcv", None, None),
            P("freq", "rcv", None, None),
        ),
        out_specs=(
            P("freq", "rcv", None, None),
            P("freq", "rcv", None, None),
            P("freq", "rcv", None, None),
            P("freq", "rcv", None, None),
            P("freq", None, None),
        ),
        check_vma=False,
    )
```

profile of v0, /device:TPU:0, one launch (start us, length us, event | category | flops | bytes accessed | tf_op | source)
XLA Modules:
  0.0 475.7 jit_solution(8466674727431938095)
XLA Ops:
  10.4 89.0 %all-gather.4.cloned.1.call-done = bf16[2,2560,2,192]{3,2,0,1:T(2,128)(2,1)} async-done(((bf16[2,320,2,192]{3,2,0,1:T(2,128)(2,1)}), bf16[2,2560,2,192]{3,2,0,1:T(2,128)(2,1)}) %all-gather.4.cloned.1.call-update) | async-done | bytes 3932176 | tf_op jit(solution)/shard_map/all_gather | solution.py:76
  99.4 8.1 %fusion.2 = f32[2,2,320,2,192]{2,4,3,1,0:T(8,128)S(1)} fusion(bf16[2,2,320,2560]{3,2,1,0:T(8,128)(2,1)} %param.6, bf16[2,2560,2,192,1]{3,2,0,1,4:T(2,128)(2,1)} %bitcast.192), kind=kOutput, calls=%fused_computation.2 | convolution fusion | flops 2516582400 | bytes 12451840 | tf_op jit(solution)/shard_map/fpnm,fmqk->fpnqk/dot_general | solution.py:72
  109.7 3.5 all-to-all-start
  117.2 13.3 %all-to-all-done = f32[2,320,2,192]{3,0,2,1:T(2,128)S(1)} async-done(((f32[2,320,2,192]{3,0,2,1:T(2,128)}), f32[2,320,2,192]{3,0,2,1:T(2,128)S(1)}, u32[]{:S(2)}, u32[]{:S(2)}) %all-to-all-start) | async-done | bytes 983072 | tf_op jit(solution)/shard_map/all_to_all | solution.py:63
  132.6 4.4 fusion.27
  137.1 4.4 fusion.26
  141.5 5.0 %subtract_select_fusion.1 = f32[64,80,192]{2,0,1:T(8,128)S(1)} fusion(f32[64,80,192]{2,0,1:T(8,128)S(1)} %fusion.27, s32[80,192]{1,0:T(8,128)S(1)} %copy.102, f32[8,80,2,192]{3,0,1,2:T(8,128)S(1)} %all_to_all.69, f32[8]{0:T(128)S(1)} %add_convert_fusion, f32[64]{0:T(128)S(1)} %iota_multiply_fusion), kind=kOutput, calls=%fused_computation.15 | convolution fusion | flops 97321984 | bytes 9913344 | tf_op jit(solution)/shard_map/tf,frk->trk/dot_general | solution.py:23
  149.2 4.9 %add_select_fusion.1 = f32[64,80,192]{2,0,1:T(8,128)S(1)} fusion(f32[64,80,192]{2,0,1:T(8,128)S(1)} %fusion.26, s32[80,192]{1,0:T(8,128)S(1)} %copy.102, f32[8,80,2,192]{3,0,1,2:T(8,128)S(1)} %all_to_all.69, f32[8]{0:T(128)S(1)} %add_convert_fusion, f32[64]{0:T(128)S(1)} %iota_multiply_fusion), kind=kOutput, calls=%fused_computation.14 | convolution fusion | flops 97321984 | bytes 9913344 | tf_op jit(solution)/shard_map/tf,frk->trk/dot_general | solution.py:23
  154.1 2.9 fusion.25
  163.8 3.5 all-to-all-start.1
  168.3 16.2 %all-to-all-done.1 = f32[8,80,2,192]{3,1,2,0:T(8,128)S(1)} async-done(((f32[8,80,2,192]{3,1,2,0:T(8,128)}), f32[8,80,2,192]{3,1,2,0:T(8,128)S(1)}, u32[]{:S(2)}, u32[]{:S(2)}) %all-to-all-start.1) | async-done | bytes 983072 | tf_op jit(solution)/shard_map/all_to_all | solution.py:69
  187.2 38.8 %all-reduce = (f32[]{:T(128)}, f32[]{:T(128)}) all-reduce(f32[]{:T(128)} %multiply_reduce_fusion.2, f32[]{:T(128)} %multiply_reduce_fusion), channel_id=1, replica_groups=mesh['freq'=4,'rcv'=8] {'freq','rcv'}, use_global_device_ids=true, to_apply=%region_1.0 | all-reduce | flops 2 | bytes 16 | tf_op jit(solution)/shard_map/psum | solution.py:78
  228.7 20.6 %all_to_all.90 = f32[2,320,2,192]{3,2,0,1:T(2,128)S(1)} all-to-all(f32[2,320,2,192]{3,2,0,1:T(2,128)S(1)} %copy.115), channel_id=1, replica_groups=mesh['freq'=4,'rcv'=8] {'freq'}, dimensions={1} | all-to-all | bytes 1966080 | tf_op jit(solution)/shard_map/all_to_all | solution.py:63
  254.2 4.4 fusion.29
  258.7 4.4 fusion.28
  263.1 5.0 %subtract_select_fusion = f32[64,80,192]{2,0,1:T(8,128)S(1)} fusion(f32[64,80,192]{2,0,1:T(8,128)S(1)} %fusion.29, s32[80,192]{1,0:T(8,128)S(1)} %copy.102, f32[8,80,2,192]{3,0,1,2:T(8,128)S(1)} %all_to_all.74, f32[8]{0:T(128)S(1)} %add_convert_fusion, f32[64]{0:T(128)S(1)} %iota_multiply_fusion), kind=kOutput, calls=%fused_computation.13 | convolution fusion | flops 97321984 | bytes 9913344 | tf_op jit(solution)/shard_map/tf,frk->trk/dot_general | solution.py:23
  270.8 4.9 %add_select_fusion = f32[64,80,192]{2,0,1:T(8,128)S(1)} fusion(f32[64,80,192]{2,0,1:T(8,128)S(1)} %fusion.28, s32[80,192]{1,0:T(8,128)S(1)} %copy.102, f32[8,80,2,192]{3,0,1,2:T(8,128)S(1)} %all_to_all.74, f32[8]{0:T(128)S(1)} %add_convert_fusion, f32[64]{0:T(128)S(1)} %iota_multiply_fusion), kind=kOutput, calls=%fused_computation.12 | convolution fusion | flops 97321984 | bytes 9913344 | tf_op jit(solution)/shard_map/tf,frk->trk/dot_general | solution.py:23
  278.3 2.8 fusion.58
  284.0 12.6 %all_to_all.91 = bf16[8,80,2,192]{3,1,2,0:T(8,128)(2,1)S(1)} all-to-all(bf16[8,80,2,192]{3,1,2,0:T(8,128)(2,1)S(1)} %copy.118), channel_id=1, replica_groups=mesh['freq'=4,'rcv'=8] {'freq'}, dimensions={0} | all-to-all | bytes 983040 | tf_op jit(solution)/shard_map/all_to_all | solution.py:69
  298.3 8.2 %fusion.4 = f32[2,2,320,2,192]{2,4,0,3,1:T(8,128)S(1)} fusion(bf16[2,2560,2,192,1]{3,2,0,1,4:T(2,128)(2,1)} %bitcast.190, bf16[2,2,320,2560]{3,2,1,0:T(8,128)(2,1)} %param.6), kind=kOutput, calls=%fused_computation.4 | convolution fusion | flops 2516582400 | bytes 12451840 | tf_op jit(solution)/shard_map/fpnm,fmqk->fpnqk/dot_general | solution.py:72
  310.4 19.7 %all_to_all.92 = f32[2,320,2,192]{3,0,2,1:T(2,128)S(1)} all-to-all(f32[2,320,2,192]{3,0,2,1:T(2,128)S(1)} %copy.131), channel_id=1, replica_groups=mesh['freq'=4,'rcv'=8] {'freq'}, dimensions={1} | all-to-all | bytes 1966080 | tf_op jit(solution)/shard_map/all_to_all | solution.py:63
  335.0 4.4 fusion.31
  339.4 4.4 fusion.30
  343.8 5.4 %subtract_multiply_fusion = f32[64,80,192]{2,0,1:T(8,128)S(1)} fusion(f32[64,80,192]{2,0,1:T(8,128)S(1)} %fusion.31, s32[80,192]{1,0:T(8,128)S(1)} %copy.102, f32[8,80,2,192]{3,0,1,2:T(8,128)S(1)} %all_to_all.79, f32[8]{0:T(128)S(1)} %add_convert_fusion, f32[64]{0:T(128)S(1)} %iota_multiply_fusion), kind=kOutput, calls=%fused_computation.10 | convolution fusion | flops 99288064 | bytes 9913344 | tf_op jit(solution)/shard_map/tf,frk->trk/dot_general | solution.py:23
  351.9 5.2 %add_multiply_fusion = f32[64,80,192]{2,0,1:T(8,128)S(1)} fusion(f32[64,80,192]{2,0,1:T(8,128)S(1)} %fusion.30, s32[80,192]{1,0:T(8,128)S(1)} %copy.102, f32[8,80,2,192]{3,0,1,2:T(8,128)S(1)} %all_to_all.79, f32[8]{0:T(128)S(1)} %add_convert_fusion, f32[64]{0:T(128)S(1)} %iota_multiply_fusion), kind=kOutput, calls=%fused_computation.9 | convolution fusion | flops 99288064 | bytes 9913344 | tf_op jit(solution)/shard_map/tf,frk->trk/dot_general | solution.py:23
  359.8 2.8 fusion.52
  362.6 2.7 fusion.15
  366.9 3.5 all-to-all-start.5
  372.5 15.1 %all-to-all-done.5 = f32[8,80,2,192]{3,1,2,0:T(8,128)S(1)} async-done(((f32[8,80,2,192]{3,1,2,0:T(8,128)}), f32[8,80,2,192]{3,1,2,0:T(8,128)S(1)}, u32[]{:S(2)}, u32[]{:S(2)}) %all-to-all-start.5) | async-done | bytes 983072 | tf_op jit(solution)/shard_map/all_to_all | solution.py:69
  390.4 10.1 %fusion.9 = f32[2,2,320,2,192]{2,4,1,3,0:T(8,128)S(1)} fusion(bf16[2,2,320,2560]{3,2,1,0:T(8,128)(2,1)} %param.6, bf16[2,2560,2,192,1]{3,2,0,1,4:T(2,128)(2,1)} %bitcast.191), kind=kOutput, calls=%fused_computation.17 | convolution fusion | flops 2516582400 | bytes 12451840 | tf_op jit(solution)/shard_map/fpnm,fmqk->fpnqk/dot_general | solution.py:72
  402.7 39.1 %psum.30 = f32[]{:T(128)} all-reduce(f32[]{:T(128)} %multiply_reduce_fusion.1), channel_id=1, replica_groups=mesh['freq'=4,'rcv'=8] {'freq','rcv'}, use_global_device_ids=true, to_apply=%region_5.0 | all-reduce | flops 1 | bytes 8 | tf_op jit(solution)/shard_map/psum | solution.py:87
  446.5 20.7 %psum.31 = f32[2,2,192]{2,0,1:T(2,128)S(1)} all-reduce(f32[2,2,192]{2,0,1:T(2,128)S(1)} %pad_maximum_fusion.5), channel_id=1, replica_groups=mesh['freq'=4,'rcv'=8] {'rcv'}, use_global_device_ids=true, to_apply=%region_8.0 | all-reduce | flops 768 | bytes 6144 | tf_op jit(solution)/shard_map/psum | solution.py:101
  (89 shorter events, 68.2 us)
Async XLA Ops:
  7.2 109.8 %copy-start = (s32[320,192]{0,1:T(8,128)S(1)}, s32[320,192]{0,1:T(8,128)}, u32[]{:S(2)}) copy-start(s32[320,192]{0,1:T(8,128)} %param.7) | copy-start | bytes 737284
  7.2 92.2 %all-gather.4.cloned.1.call-start = ((), (), s32[]{:S(2)}) async-start(), calls=%async_computation.6 | async-start | bytes 5898240 | tf_op jit(solution)/shard_map/all_gather | solution.py:76
  107.6 9.2 %copy-start.2 = (f32[2,320,1,192]{1,3,0,2:T(8,128)}, f32[2,320,1,192]{1,3,0,2:T(8,128)S(1)}, u32[]{:S(2)}) copy-start(f32[2,320,1,192]{1,3,0,2:T(8,128)S(1)} %fusion.39) | copy-start | bytes 1474564
  109.7 20.8 %all-to-all-start = ((f32[2,320,2,192]{3,0,2,1:T(2,128)}), f32[2,320,2,192]{3,0,2,1:T(2,128)S(1)}, u32[]{:S(2)}, u32[]{:S(2)}) async-start(f32[2,320,2,192]{3,0,2,1:T(2,128)} %copy.107), calls=%async_computation | async-start | bytes 2621440 | tf_op jit(solution)/shard_map/all_to_all | solution.py:63
  113.3 185.0 %all-gather.8.cloned.1.call-start = ((), (), s32[]{:S(2)}) async-start(), calls=%async_computation.8 | async-start | bytes 5898240 | tf_op jit(solution)/shard_map/all_gather | solution.py:89
  162.2 5.2 %copy-start.8 = (f32[2,320,2,192]{1,3,2,0:T(8,128)S(1)}, f32[2,320,2,192]{1,3,2,0:T(8,128)}, u32[]{:S(2)}) copy-start(f32[2,320,2,192]{1,3,2,0:T(8,128)} %param.11) | copy-start | bytes 2949124
  163.8 20.8 %all-to-all-start.1 = ((f32[8,80,2,192]{3,1,2,0:T(8,128)}), f32[8,80,2,192]{3,1,2,0:T(8,128)S(1)}, u32[]{:S(2)}, u32[]{:S(2)}) async-start(f32[8,80,2,192]{3,1,2,0:T(8,128)} %copy.110), calls=%async_computation.1 | async-start | bytes 2621440 | tf_op jit(solution)/shard_map/all_to_all | solution.py:69
  167.4 223.1 %all-gather.6.cloned.1.call-start = ((), (), s32[]{:S(2)}) async-start(), calls=%async_computation.7 | async-start | bytes 5898240 | tf_op jit(solution)/shard_map/all_gather | solution.py:85
  298.3 8.3 %copy-start.3 = (f32[2,320,1,192]{1,3,0,2:T(8,128)S(1)}, f32[2,320,1,192]{1,3,0,2:T(8,128)}, u32[]{:S(2)}) copy-start(f32[2,320,1,192]{1,3,0,2:T(8,128)} %copy-done.2) | copy-start | bytes 1474564
  366.9 20.8 %all-to-all-start.5 = ((f32[8,80,2,192]{3,1,2,0:T(8,128)}), f32[8,80,2,192]{3,1,2,0:T(8,128)S(1)}, u32[]{:S(2)}, u32[]{:S(2)}) async-start(f32[8,80,2,192]{3,1,2,0:T(8,128)} %copy.134), calls=%async_computation.5 | async-start | bytes 2621440 | tf_op jit(solution)/shard_map/all_to_all | solution.py:69
  400.6 41.9 %copy-start.4 = (f32[2,320,2,192]{1,3,2,0:T(8,128)S(1)}, f32[2,320,2,192]{1,3,2,0:T(8,128)}, u32[]{:S(2)}) copy-start(f32[2,320,2,192]{1,3,2,0:T(8,128)} %param.10) | copy-start | bytes 2949124
  402.7 43.4 %copy-start.6 = (f32[2,320,1,192]{1,3,0,2:T(8,128)S(1)}, f32[2,320,1,192]{1,3,0,2:T(8,128)}, u32[]{:S(2)}) copy-start(f32[2,320,1,192]{1,3,0,2:T(8,128)} %copy.160) | copy-start | bytes 1474564
  441.8 27.1 %copy-start.1 = (s32[320,192]{0,1:T(8,128)S(1)}, s32[320,192]{0,1:T(8,128)}, u32[]{:S(2)}) copy-start(s32[320,192]{0,1:T(8,128)} %param.7) | copy-start | bytes 737284
  442.5 3.6 copy-start.7
  445.1 22.7 %copy-start.5 = (f32[2,320,2,192]{1,3,0,2:T(8,128)S(1)}, f32[2,320,2,192]{1,3,0,2:T(8,128)}, u32[]{:S(2)}) copy-start(f32[2,320,2,192]{1,3,0,2:T(8,128)} %get-tuple-element.33) | copy-start | bytes 2949124
Sparse Core Ops, SparseCore 0:
  10.7 88.5 all-gather.3
  117.0 84.5 all-gather.7
  298.4 84.9 all-gather.5
where the time goes:
time: 480 us; the launch traced here: 476 us
  blocking collectives  151 us (31%)
  waiting for transfers between devices  134 us (28%)
  matrix products  116 us (24%)
  local copies, waits for them, and re-layouts  36.4 us (8%)
  between operations  17.1 us (4%)
  starting transfers between devices  10.7 us (2%)
  other arithmetic  10.5 us (2%)
    all_gather x1, waiting for transfers between devices, per_device(): lax.all_gather(direction_low, 'rcv', axis=1, tiled=True)  89 us
    dot_general x12, matrix products, contract_time(): return jnp.einsum('tf,frk->trk', table, values, precision=highest)  57 us
    all_to_all x2, blocking collectives, gate(): lax.all_to_all(field, 'freq', split_axis=1, concat_axis=0, tiled=True)  40.3 us
    psum x1, blocking collectives, per_device(): new_gamma = lax.psum(jnp.sum(new_gradient * new_gradient), ('freq', 'rcv'))  39.1 us
    psum x1, blocking collectives, per_device(): gamma = lax.psum(jnp.sum(gradient * gradient), ('freq', 'rcv'))  38.8 us
    dot_general x12, matrix products, contract_back(): return jnp.einsum('tf,trk->frk', table, values, precision=highest)  32.3 us
    all_to_all x2, waiting for transfers between devices, gate(): lax.all_to_all(gated_part, 'freq', split_axis=0, concat_axis=1, tiled=True)  31.3 us
    dot_general x3, matrix products, accumulate(): jnp.einsum('fpnm,fmqk->fpnqk', reflection, piece, preferred_element_type=...  26.4 us
  transfers between devices with their start and end apart: 6, of which 4 were waited for; matrix products, arithmetic and copies ran while one was open for 26% of the time, Pallas kernels for 0%

commit v1 on v0

--- a/solution.py
+++ b/solution.py
@@ -10,6 +10,22 @@
 band_start = 5
 tiny = 1e-06
 highest = lax.Precision.HIGHEST
+
+
+def swapped_with_each(shard, axis, split, join):
+    ways, here = (lax.axis_size(axis), lax.axis_index(axis))
+    width = shard.shape[split] // ways
+    dims = list(shard.shape)
+    dims[split] = width
+    height = dims[join]
+    dims[join] = height * ways
+    full = jnp.zeros(dims, shard.dtype)
+    for mask in range(ways):
+        part = lax.dynamic_slice_in_dim(shard, (here ^ mask) * width, width, axis=split)
+        if mask:
+            part = lax.ppermute(part, axis, [(d, d ^ mask) for d in range(ways)])
+        full = lax.dynamic_update_slice_in_dim(full, part, (here ^ mask) * height, axis=join)
+    return full
 
 
 def tables(count):
@@ -60,7 +76,7 @@
     cos_table, sin_table = tables(F)
 
     def gate(field, complement):
-        spread = lax.all_to_all(field, "freq", split_axis=1, concat_axis=0, tiled=True)
+        spread = swapped_with_each(field, "freq", 1, 0)
         share = local_rows // groups
         limits = lax.dynamic_slice_in_dim(starts, position * share, share, 0)
         gated_part = time_gate(

time: 480 us -> 498 us (1.038)
  waiting for transfers between devices: 134 us -> 179 us
  blocking collectives: 151 us -> 112 us
    all_to_all x2 -> x0, blocking collectives: 40.3 us -> none  [gate(): lax.all_to_all(field, 'freq', split_axis=1, concat_axis=0, tiled=True)]
    ppermute x0 -> x9, waiting for transfers between devices: none -> 31 us  [swapped_with_each(): part = lax.ppermute(part, axis, [(d, d ^ mask) for d in range(ways)])]
    all_gather x1, waiting for transfers between devices: 0.01 us -> 28.6 us  [per_device(): total = accumulate(lax.all_gather(gated, 'rcv', axis=1, tiled=True))]
    all_gather x1, waiting for transfers between devices: 0.02 us -> 19.8 us  [per_device(): lax.all_gather(focusing_low, 'rcv', axis=1, tiled=True)]
    all_to_all x2, waiting for transfers between devices: 31.3 us -> 14.4 us  [gate(): lax.all_to_all(gated_part, 'freq', split_axis=0, concat_axis=1, tiled=True)]
    all_to_all x1 -> x0, waiting for transfers between devices: 13.3 us -> none  [gate(): lax.all_to_all(field, 'freq', split_axis=1, concat_axis=0, tiled=True)]
    all_to_all x9 -> x0, local copies, waits for them, and re-layouts: 12 us -> none  [gate(): lax.all_to_all(field, 'freq', split_axis=1, concat_axis=0, tiled=True)]
    ppermute x0 -> x6, local copies, waits for them, and re-layouts: none -> 7.91 us  [swapped_with_each(): part = lax.ppermute(part, axis, [(d, d ^ mask) for d in range(ways)])]
  transfers between devices with their start and end apart: 6 -> 14, of which waited for: 4 -> 10; matrix products, arithmetic and copies ran while one was open for 26% -> 22% of each run, Pallas kernels for 0% -> 0%
where the time goes in v1:
time: 498 us; the launch traced here: 493 us
  waiting for transfers between devices  179 us (36%)
  matrix products  117 us (23%)
  blocking collectives  112 us (22%)
  local copies, waits for them, and re-layouts  41.2 us (8%)
  between operations  17.2 us (3%)
  starting transfers between devices  13.7 us (3%)
  other arithmetic  13.5 us (3%)
    all_gather x1, waiting for transfers between devices, per_device(): lax.all_gather(direction_low, 'rcv', axis=1, tiled=True)  85.3 us
    dot_general x12, matrix products, contract_time(): return jnp.einsum('tf,frk->trk', table, values, precision=highest)  57.3 us
    psum x1, blocking collectives, per_device(): gamma = lax.psum(jnp.sum(gradient * gradient), ('freq', 'rcv'))  39 us
    psum x1, blocking collectives, per_device(): new_gamma = lax.psum(jnp.sum(new_gradient * new_gradient), ('freq', 'rcv'))  38.6 us
    dot_general x12, matrix products, contract_back(): return jnp.einsum('tf,trk->frk', table, values, precision=highest)  32.1 us
    ppermute x9, waiting for transfers between devices, swapped_with_each(): part = lax.ppermute(part, axis, [(d, d ^ mask) for d in range(ways)])  31 us
    all_gather x1, waiting for transfers between devices, per_device(): total = accumulate(lax.all_gather(gated, 'rcv', axis=1, tiled=True))  28.6 us
    dot_general x3, matrix products, accumulate(): jnp.einsum('fpnm,fmqk->fpnqk', reflection, piece, preferred_element_type=...  27.3 us
  transfers between devices with their start and end apart: 14, of which 10 were waited for; matrix products, arithmetic and copies ran while one was open for 22% of the time, Pallas kernels for 0%

profile of v1, /device:TPU:0, one launch (start us, length us, event | category | flops | bytes accessed | tf_op | source)
XLA Modules:
  0.0 493.4 jit_solution(13444730835810371648)
XLA Ops:
  14.1 85.3 %all-gather.4.cloned.1.call-done = bf16[2,2560,2,192]{3,2,0,1:T(2,128)(2,1)} async-done(((bf16[2,320,2,192]{3,2,0,1:T(2,128)(2,1)}), bf16[2,2560,2,192]{3,2,0,1:T(2,128)(2,1)}) %all-gather.4.cloned.1.call-update) | async-done | bytes 3932176 | tf_op jit(solution)/shard_map/all_gather | solution.py:92
  99.4 8.1 %fusion.2 = f32[2,2,320,2,192]{2,4,3,1,0:T(8,128)S(1)} fusion(bf16[2,2,320,2560]{3,2,1,0:T(8,128)(2,1)} %param.6, bf16[2,2560,2,192,1]{3,2,0,1,4:T(2,128)(2,1)} %bitcast.173), kind=kOutput, calls=%fused_computation.2 | convolution fusion | flops 2516582400 | bytes 12451840 | tf_op jit(solution)/shard_map/fpnm,fmqk->fpnqk/dot_general | solution.py:88
  115.3 5.8 %collective-permute-done.1 = f32[2,80,2,192]{1,3,0,2:T(8,128)} collective-permute-done((f32[2,80,2,192]{1,3,0,2:T(8,128)S(1)}, f32[2,80,2,192]{1,3,0,2:T(8,128)}, u32[]{:S(2)}, u32[]{:S(2)}) %collective-permute-start.1) | collective-permute-done | bytes 245792 | tf_op jit(solution)/shard_map/ppermute | solution.py:26
  122.4 6.3 %collective-permute-done.2 = f32[2,80,2,192]{1,3,0,2:T(8,128)} collective-permute-done((f32[2,80,2,192]{1,3,0,2:T(8,128)}, f32[2,80,2,192]{1,3,0,2:T(8,128)}, u32[]{:S(2)}, u32[]{:S(2)}) %collective-permute-start.2) | collective-permute-done | bytes 245792 | tf_op jit(solution)/shard_map/ppermute | solution.py:26
  131.8 4.4 fusion.29
  136.2 4.4 fusion.28
  140.6 5.1 %subtract_select_fusion.1 = f32[64,80,192]{2,0,1:T(8,128)S(1)} fusion(f32[64,80,192]{2,0,1:T(8,128)S(1)} %fusion.29, s32[80,192]{1,0:T(8,128)S(1)} %copy.111, f32[8,80,2,192]{3,0,1,2:T(8,128)S(1)} %constant_dynamic-update-slice_fusion.7, f32[8]{0:T(128)S(1)} %add_convert_fusion, f32[64]{0:T(128)S(1)} %iota_multiply_fusion), kind=kOutput, calls=%fused_computation.15 | convolution fusion | flops 97321984 | bytes 9913344 | tf_op jit(solution)/shard_map/tf,frk->trk/dot_general | solution.py:39
  148.3 4.9 add_select_fusion.1
  155.9 2.8 fusion.70
  162.9 3.5 all-to-all-start
  166.5 19.8 %all-gather.8.cloned.1.call-done = bf16[2,2560,2,192]{3,2,0,1:T(2,128)(2,1)} async-done(((bf16[2,320,2,192]{3,2,0,1:T(2,128)(2,1)}), bf16[2,2560,2,192]{3,2,0,1:T(2,128)(2,1)}) %all-gather.8.cloned.1.call-update) | async-done | bytes 3932176 | tf_op jit(solution)/shard_map/all_gather | solution.py:105
  186.2 9.1 %fusion.4 = f32[2,2,320,2,192]{2,4,0,3,1:T(8,128)} fusion(bf16[2,2560,2,192,1]{3,2,0,1,4:T(2,128)(2,1)} %bitcast.172, bf16[2,2,320,2560]{3,2,1,0:T(8,128)(2,1)} %param.6), kind=kOutput, calls=%fused_computation.4 | convolution fusion | flops 2516582400 | bytes 12451840 | tf_op jit(solution)/shard_map/fpnm,fmqk->fpnqk/dot_general | solution.py:88
  198.8 39.0 %all-reduce = (f32[]{:T(128)}, f32[]{:T(128)}) all-reduce(f32[]{:T(128)} %multiply_reduce_fusion.2, f32[]{:T(128)} %multiply_reduce_fusion), channel_id=1, replica_groups=mesh['freq'=4,'rcv'=8] {'freq','rcv'}, use_global_device_ids=true, to_apply=%region_1.0 | all-reduce | flops 2 | bytes 16 | tf_op jit(solution)/shard_map/psum | solution.py:94
  256.2 6.5 %collective-permute-done.8 = f32[2,80,2,192]{1,3,0,2:T(8,128)} collective-permute-done((f32[2,80,2,192]{1,3,0,2:T(8,128)}, f32[2,80,2,192]{1,3,0,2:T(8,128)}, u32[]{:S(2)}, u32[]{:S(2)}) %collective-permute-start.8) | collective-permute-done | bytes 245792 | tf_op jit(solution)/shard_map/ppermute | solution.py:26
  265.1 5.1 %collective-permute-done.4 = f32[2,80,2,192]{3,0,1,2:T(2,128)} collective-permute-done((f32[2,80,2,192]{3,0,1,2:T(2,128)}, f32[2,80,2,192]{3,0,1,2:T(2,128)}, u32[]{:S(2)}, u32[]{:S(2)}) %collective-permute-start.4) | collective-permute-done | bytes 245792 | tf_op jit(solution)/shard_map/ppermute | solution.py:26
  271.4 5.3 %collective-permute-done.5 = f32[2,80,2,192]{3,0,1,2:T(2,128)} collective-permute-done((f32[2,80,2,192]{3,0,1,2:T(2,128)}, f32[2,80,2,192]{3,0,1,2:T(2,128)}, u32[]{:S(2)}, u32[]{:S(2)}) %collective-permute-start.5) | collective-permute-done | bytes 245792 | tf_op jit(solution)/shard_map/ppermute | solution.py:26
  278.1 4.4 fusion.31
  282.5 4.6 fusion.30
  287.2 4.9 subtract_select_fusion
  294.7 5.1 %add_select_fusion = f32[64,80,192]{2,0,1:T(8,128)S(1)} fusion(f32[64,80,192]{2,0,1:T(8,128)S(1)} %fusion.30, s32[80,192]{1,0:T(8,128)S(1)} %copy.111, f32[8,80,2,192]{3,0,1,2:T(8,128)S(1)} %get-tuple-element.47, f32[8]{0:T(128)S(1)} %add_convert_fusion, f32[64]{0:T(128)S(1)} %iota_multiply_fusion), kind=kOutput, calls=%fused_computation.12 | convolution fusion | flops 97321984 | bytes 9913344 | tf_op jit(solution)/shard_map/tf,frk->trk/dot_general | solution.py:39
  307.9 12.8 %all_to_all.36 = bf16[8,80,2,192]{3,1,2,0:T(8,128)(2,1)S(1)} all-to-all(bf16[8,80,2,192]{3,1,2,0:T(8,128)(2,1)S(1)} %copy.125), channel_id=1, replica_groups=mesh['freq'=4,'rcv'=8] {'freq'}, dimensions={0} | all-to-all | bytes 983040 | tf_op jit(solution)/shard_map/all_to_all | solution.py:85
  322.3 4.4 fusion.33
  326.7 4.4 fusion.32
  331.1 5.4 %subtract_multiply_fusion = f32[64,80,192]{2,0,1:T(8,128)S(1)} fusion(f32[64,80,192]{2,0,1:T(8,128)S(1)} %fusion.33, s32[80,192]{1,0:T(8,128)S(1)} %copy.111, f32[8,80,2,192]{3,0,1,2:T(8,128)S(1)} %get-tuple-element.48, f32[8]{0:T(128)S(1)} %add_convert_fusion, f32[64]{0:T(128)S(1)} %iota_multiply_fusion), kind=kOutput, calls=%fused_computation.10 | convolution fusion | flops 99288064 | bytes 9913344 | tf_op jit(solution)/shard_map/tf,frk->trk/dot_general | solution.py:39
  339.2 5.2 %add_multiply_fusion = f32[64,80,192]{2,0,1:T(8,128)S(1)} fusion(f32[64,80,192]{2,0,1:T(8,128)S(1)} %fusion.32, s32[80,192]{1,0:T(8,128)S(1)} %copy.111, f32[8,80,2,192]{3,0,1,2:T(8,128)S(1)} %get-tuple-element.48, f32[8]{0:T(128)S(1)} %add_convert_fusion, f32[64]{0:T(128)S(1)} %iota_multiply_fusion), kind=kOutput, calls=%fused_computation.9 | convolution fusion | flops 99288064 | bytes 9913344 | tf_op jit(solution)/shard_map/tf,frk->trk/dot_general | solution.py:39
  347.1 2.8 fusion.58
  354.2 3.7 all-to-all-start.2
  360.7 14.4 %all-to-all-done.2 = f32[8,80,2,192]{3,1,2,0:T(8,128)S(1)} async-done(((f32[8,80,2,192]{3,1,2,0:T(8,128)}), f32[8,80,2,192]{3,1,2,0:T(8,128)S(1)}, u32[]{:S(2)}, u32[]{:S(2)}) %all-to-all-start.2) | async-done | bytes 983072 | tf_op jit(solution)/shard_map/all_to_all | solution.py:85
  378.7 28.6 %all-gather.6.cloned.1.call-done = bf16[2,2560,2,192]{3,2,0,1:T(2,128)(2,1)} async-done(((bf16[2,320,2,192]{3,2,0,1:T(2,128)(2,1)}), bf16[2,2560,2,192]{3,2,0,1:T(2,128)(2,1)}) %all-gather.6.cloned.1.call-update) | async-done | bytes 3932176 | tf_op jit(solution)/shard_map/all_gather | solution.py:101
  407.3 10.1 %fusion.9 = f32[2,2,320,2,192]{2,4,1,3,0:T(8,128)S(1)} fusion(bf16[2,2,320,2560]{3,2,1,0:T(8,128)(2,1)} %param.6, bf16[2,2560,2,192,1]{3,2,0,1,4:T(2,128)(2,1)} %bitcast.174), kind=kOutput, calls=%fused_computation.26 | convolution fusion | flops 2516582400 | bytes 12451840 | tf_op jit(solution)/shard_map/fpnm,fmqk->fpnqk/dot_general | solution.py:88
  419.7 38.6 %psum.30 = f32[]{:T(128)} all-reduce(f32[]{:T(128)} %multiply_reduce_fusion.1), channel_id=1, replica_groups=mesh['freq'=4,'rcv'=8] {'freq','rcv'}, use_global_device_ids=true, to_apply=%region_5.0 | all-reduce | flops 1 | bytes 8 | tf_op jit(solution)/shard_map/psum | solution.py:103
  463.4 21.5 %psum.31 = f32[2,2,192]{2,0,1:T(2,128)S(1)} all-reduce(f32[2,2,192]{2,0,1:T(2,128)S(1)} %pad_maximum_fusion.5), channel_id=1, replica_groups=mesh['freq'=4,'rcv'=8] {'rcv'}, use_global_device_ids=true, to_apply=%region_8.0 | all-reduce | flops 768 | bytes 6144 | tf_op jit(solution)/shard_map/psum | solution.py:117
  (128 shorter events, 89.7 us)
Async XLA Ops:
  7.2 5.3 %copy-start = (s32[320,192]{0,1:T(8,128)S(1)}, s32[320,192]{0,1:T(8,128)}, u32[]{:S(2)}) copy-start(s32[320,192]{0,1:T(8,128)} %param.7) | copy-start | bytes 737284
  7.2 92.2 %all-gather.4.cloned.1.call-start = ((), (), s32[]{:S(2)}) async-start(), calls=%async_computation.3 | async-start | bytes 5898240 | tf_op jit(solution)/shard_map/all_gather | solution.py:92
  8.6 1.9 copy-start.6
  10.4 175.8 %all-gather.8.cloned.1.call-start = ((), (), s32[]{:S(2)}) async-start(), calls=%async_computation.5 | async-start | bytes 5898240 | tf_op jit(solution)/shard_map/all_gather | solution.py:105
  10.6 2.6 copy-start.12
  107.6 3.3 copy-start.14
  107.7 3.4 copy-start.13
  109.1 5.0 %collective-permute-start = (f32[2,80,2,192]{1,3,0,2:T(8,128)}, f32[2,80,2,192]{1,3,0,2:T(8,128)}, u32[]{:S(2)}, u32[]{:S(2)}) collective-permute-start(f32[2,80,2,192]{1,3,0,2:T(8,128)} %get-tuple-element.45), channel_id=1, source_target_pairs={{0,8},{8,0},{16,24},{24,16},{1,9},{9,1},{17,25},{25,17},{2,10},{10... | collective-permute-start | bytes 737288 | tf_op jit(solution)/shard_map/ppermute | solution.py:26
  109.1 12.1 %collective-permute-start.1 = (f32[2,80,2,192]{1,3,0,2:T(8,128)S(1)}, f32[2,80,2,192]{1,3,0,2:T(8,128)}, u32[]{:S(2)}, u32[]{:S(2)}) collective-permute-start(f32[2,80,2,192]{1,3,0,2:T(8,128)S(1)} %get-tuple-element.46), channel_id=1, source_target_pairs={{0,16},{8,24},{16,0},{24,8},{1,17},{9,25},{17,1},{25,9},{2,18},{10... | collective-permute-start | bytes 737288 | tf_op jit(solution)/shard_map/ppermute | solution.py:26
  110.5 18.1 %collective-permute-start.2 = (f32[2,80,2,192]{1,3,0,2:T(8,128)}, f32[2,80,2,192]{1,3,0,2:T(8,128)}, u32[]{:S(2)}, u32[]{:S(2)}) collective-permute-start(f32[2,80,2,192]{1,3,0,2:T(8,128)} %get-tuple-element.43), channel_id=1, source_target_pairs={{0,24},{8,16},{16,8},{24,0},{1,25},{9,17},{17,9},{25,1},{2,26},{10... | collective-permute-start | bytes 737288 | tf_op jit(solution)/shard_map/ppermute | solution.py:26
  130.6 1.0 copy-start.11
  162.9 32.4 %all-to-all-start = ((f32[8,80,2,192]{3,1,2,0:T(8,128)}), f32[8,80,2,192]{3,1,2,0:T(8,128)S(1)}, u32[]{:S(2)}, u32[]{:S(2)}) async-start(f32[8,80,2,192]{3,1,2,0:T(8,128)} %copy.120), calls=%async_computation | async-start | bytes 2621440 | tf_op jit(solution)/shard_map/all_to_all | solution.py:85
  166.4 240.8 %all-gather.6.cloned.1.call-start = ((), (), s32[]{:S(2)}) async-start(), calls=%async_computation.4 | async-start | bytes 5898240 | tf_op jit(solution)/shard_map/all_gather | solution.py:101
  242.0 8.5 %collective-permute-start.6 = (f32[2,80,2,192]{1,3,0,2:T(8,128)}, f32[2,80,2,192]{1,3,0,2:T(8,128)S(1)}, u32[]{:S(2)}, u32[]{:S(2)}) collective-permute-start(f32[2,80,2,192]{1,3,0,2:T(8,128)} %get-tuple-element.39), channel_id=1, source_target_pairs={{0,8},{8,0},{16,24},{24,16},{1,9},{9,1},{17,25},{25,17},{2,10},{10... | collective-permute-start | bytes 737288 | tf_op jit(solution)/shard_map/ppermute | solution.py:26
  242.1 12.6 %collective-permute-start.7 = (f32[2,80,2,192]{1,3,0,2:T(8,128)}, f32[2,80,2,192]{1,3,0,2:T(8,128)}, u32[]{:S(2)}, u32[]{:S(2)}) collective-permute-start(f32[2,80,2,192]{1,3,0,2:T(8,128)} %get-tuple-element.38), channel_id=1, source_target_pairs={{0,16},{8,24},{16,0},{24,8},{1,17},{9,25},{17,1},{25,9},{2,18},{10... | collective-permute-start | bytes 737288 | tf_op jit(solution)/shard_map/ppermute | solution.py:26
  244.4 18.3 %collective-permute-start.8 = (f32[2,80,2,192]{1,3,0,2:T(8,128)}, f32[2,80,2,192]{1,3,0,2:T(8,128)}, u32[]{:S(2)}, u32[]{:S(2)}) collective-permute-start(f32[2,80,2,192]{1,3,0,2:T(8,128)} %get-tuple-element.37), channel_id=1, source_target_pairs={{0,24},{8,16},{16,8},{24,0},{1,25},{9,17},{17,9},{25,1},{2,26},{10... | collective-permute-start | bytes 737288 | tf_op jit(solution)/shard_map/ppermute | solution.py:26
  244.6 1.3 copy-start.4
  246.6 1.4 copy-start.2
  248.1 15.8 %collective-permute-start.3 = (f32[2,80,2,192]{3,0,1,2:T(2,128)}, f32[2,80,2,192]{3,0,1,2:T(2,128)}, u32[]{:S(2)}, u32[]{:S(2)}) collective-permute-start(f32[2,80,2,192]{3,0,1,2:T(2,128)} %get-tuple-element.35), channel_id=1, source_target_pairs={{0,8},{8,0},{16,24},{24,16},{1,9},{9,1},{17,25},{25,17},{2,10},{10... | collective-permute-start | bytes 737288 | tf_op jit(solution)/shard_map/ppermute | solution.py:26
  248.2 21.9 %collective-permute-start.4 = (f32[2,80,2,192]{3,0,1,2:T(2,128)}, f32[2,80,2,192]{3,0,1,2:T(2,128)}, u32[]{:S(2)}, u32[]{:S(2)}) collective-permute-start(f32[2,80,2,192]{3,0,1,2:T(2,128)} %get-tuple-element.34), channel_id=1, source_target_pairs={{0,16},{8,24},{16,0},{24,8},{1,17},{9,25},{17,1},{25,9},{2,18},{10... | collective-permute-start | bytes 737288 | tf_op jit(solution)/shard_map/ppermute | solution.py:26
  250.5 0.7 copy-start.15
  251.3 25.4 %collective-permute-start.5 = (f32[2,80,2,192]{3,0,1,2:T(2,128)}, f32[2,80,2,192]{3,0,1,2:T(2,128)}, u32[]{:S(2)}, u32[]{:S(2)}) collective-permute-start(f32[2,80,2,192]{3,0,1,2:T(2,128)} %get-tuple-element.33), channel_id=1, source_target_pairs={{0,24},{8,16},{16,8},{24,0},{1,25},{9,17},{17,9},{25,1},{2,26},{10... | collective-permute-start | bytes 737288 | tf_op jit(solution)/shard_map/ppermute | solution.py:26
  354.2 4.3 copy-start.3
  354.2 20.9 %all-to-all-start.2 = ((f32[8,80,2,192]{3,1,2,0:T(8,128)}), f32[8,80,2,192]{3,1,2,0:T(8,128)S(1)}, u32[]{:S(2)}, u32[]{:S(2)}) async-start(f32[8,80,2,192]{3,1,2,0:T(8,128)} %copy.142), calls=%async_computation.2 | async-start | bytes 2621440 | tf_op jit(solution)/shard_map/all_to_all | solution.py:85
  417.5 1.1 copy-start.8
  417.6 41.3 %copy-start.5 = (f32[2,320,2,192]{1,3,2,0:T(8,128)S(1)}, f32[2,320,2,192]{1,3,2,0:T(8,128)}, u32[]{:S(2)}) copy-start(f32[2,320,2,192]{1,3,2,0:T(8,128)} %param.10) | copy-start | bytes 2949124
  461.4 1.3 copy-start.9
  461.4 1.7 copy-start.10
  463.1 22.4 %copy-start.7 = (f32[2,320,2,192]{1,3,0,2:T(8,128)S(1)}, f32[2,320,2,192]{1,3,0,2:T(8,128)}, u32[]{:S(2)}) copy-start(f32[2,320,2,192]{1,3,0,2:T(8,128)} %get-tuple-element.41) | copy-start | bytes 2949124
  463.1 23.5 %copy-start.1 = (s32[320,192]{0,1:T(8,128)S(1)}, s32[320,192]{0,1:T(8,128)}, u32[]{:S(2)}) copy-start(s32[320,192]{0,1:T(8,128)} %param.7) | copy-start | bytes 737284
Sparse Core Ops, SparseCore 0:
  10.7 88.5 all-gather.3
  102.1 84.0 all-gather.7
  322.4 84.8 all-gather.5
